TPU v7x, 128 devices: a whole 4x4x4 slice. The times are simulated.
128 devices in a mesh: row: 8 (over y, z_hi), col: 16 (over z_lo, x, core).
Axes of the slice: x: 4, y: 4, z: 4 (z_hi: 2, z_lo: 2; z = z_hi * 2 + z_lo), core: 2. Of those that a mesh axis runs over, the one named last changes fastest.
Arguments:
- measurement_tiling_settings: bfloat16 [65536, 40], P(('row', 'col')), may hold values from -4.875 to 4.875
- dest: int32 [65536], P(('row', 'col')), may hold values from 0 to 65535, as said below
- column_tiling_settings: bfloat16 [32768, 40], P('col'), may hold values from -4.875 to 4.875
- entry_layer_weight: bfloat16 [40, 2048], replicated, may hold values from -1 to 1
- entry_layer_bias: float32 [2048], replicated, may hold values from -3 to 3
- middle_layer_weight: bfloat16 [2048, 2048], replicated, may hold values from -0.1875 to 0.1875
- middle_layer_bias: float32 [2048], replicated, may hold values from -3 to 3
- output_layer_weight: bfloat16 [2048, 256], replicated, may hold values from -0.1875 to 0.1875
- relevance_weight_vector: float32 [256], replicated, may hold values from 0.015625 to 0.03125
- probes: float32 [32768, 64], P('col'), may hold values from -1.3258252 to 1.3258252
Outputs:
- product: float32 [65536, 64], P(('row', 'col'))
Inputs may be any that keep to these rules, and one draw needn't show every extreme that they name: dest is a permutation of 0 to 65535, and the measurements held by one device go in equal numbers to the row positions of every device, 4 to each.
All inputs are finite; a program needn't handle non-finite values.
Results may differ from a plain program's by a relative error of at most 0.0088.
Values may be sent and summed in bfloat16 or wider, within the bound.
No kernel may reach another device: no remote copies, remote signals or barrier semaphores. Data moves between devices by JAX's collectives and lax.ppermute only.
A program may use at most 64 MiB of HBM per device.

v0:
```python
import jax
import jax.numpy as jnp
from jax import lax
from jax.sharding import PartitionSpec as P


def feature_extractor(inputs, network_weight_list):
    (
        entry_layer_weight,
        entry_layer_bias,
        middle_layer_weight,
        middle_layer_bias,
        output_layer_weight,
    ) = network_weight_list
    hidden = jnp.maximum(
        jnp.dot(inputs, entry_layer_weight, preferred_element_type=jnp.float32) + entry_layer_bias,
        0.0,
    ).astype(jnp.bfloat16)
    hidden = jnp.maximum(
        jnp.dot(hidden, middle_layer_weight, preferred_element_type=jnp.float32)
        + middle_layer_bias,
        0.0,
    ).astype(jnp.bfloat16)
    return jnp.dot(hidden, output_layer_weight, preferred_element_type=jnp.float32).astype(
        jnp.bfloat16
    )


def per_device(
    measurement_tiling_settings,
    dest,
    column_tiling_settings,
    entry_layer_weight,
    entry_layer_bias,
    middle_layer_weight,
    middle_layer_bias,
    output_layer_weight,
    relevance_weight_vector,
    probes,
):
    network_weight_list = (
        entry_layer_weight,
        entry_layer_bias,
        middle_layer_weight,
        middle_layer_bias,
        output_layer_weight,
    )
    sorting_permutation = jnp.argsort(dest)
    sent_ids = dest[sorting_permutation]
    feature_matrix = feature_extractor(measurement_tiling_settings, network_weight_list)[
        sorting_permutation
    ]
    got_feats, got_ids = (
        lax.all_to_all(feature_matrix, ("row", "col"), split_axis=0, concat_axis=0, tiled=True),
        lax.all_to_all(sent_ids, ("row", "col"), split_axis=0, concat_axis=0, tiled=True),
    )
    placed = got_feats[jnp.argsort(got_ids)]
    row_feature_matrix = lax.all_gather(placed, "col", axis=0, tiled=True)
    row_total = row_feature_matrix.shape[0]
    block_rows = min(512, row_total)
    blocks = row_total // block_rows
    row_float = row_feature_matrix.astype(jnp.float32)
    scaled = (
        (row_float * relevance_weight_vector)
        .astype(jnp.bfloat16)
        .reshape(blocks, block_rows, row_feature_matrix.shape[1])
    )
    sq_row = jnp.sum(relevance_weight_vector * jnp.square(row_float), axis=1).reshape(
        blocks, block_rows
    )
    col_share = column_tiling_settings.shape[0] // lax.axis_size("row")
    own_cols = lax.dynamic_slice_in_dim(
        column_tiling_settings, lax.axis_index("row") * col_share, col_share, 0
    )
    col_feats = feature_extractor(own_cols, network_weight_list)
    empty = jnp.zeros((row_total, probes.shape[1]), jnp.float32)
    piece = lax.all_gather(col_feats, "row", axis=0, tiled=True)
    sq_col = jnp.sum(relevance_weight_vector * jnp.square(piece.astype(jnp.float32)), axis=1)

    def one_block(pieces):
        scaled_rows, sq_rows = pieces
        cross = lax.dot_general(
            scaled_rows, piece, (((1,), (1,)), ((), ())), preferred_element_type=jnp.float32
        )
        kern = jnp.exp(-0.5 * (sq_rows[:, None] + sq_col[None, :] - 2.0 * cross))
        return jnp.dot(
            kern, probes, precision=lax.Precision.HIGHEST, preferred_element_type=jnp.float32
        )

    added = lax.map(one_block, (scaled, sq_row))
    partial_sums = added.reshape(empty.shape)
    return lax.psum_scatter(partial_sums, "col", scatter_dimension=0, tiled=True)


def solution(mesh):
    placed = (
        P(("row", "col"), None),
        P(("row", "col")),
        P("col", None),
        P(),
        P(),
        P(),
        P(),
        P(),
        P(),
        P("col", None),
    )
    return jax.shard_map(
        per_device, mesh=mesh, in_specs=placed, out_specs=P(("row", "col"), None), check_vma=False
    )
```

profile of v0, /device:TPU:0, one launch (start us, length us, event | category | flops | bytes accessed | tf_op | source)
XLA Modules:
  0.0 354.9 jit_solution(17135379891913946250)
XLA Ops:
  6.5 6.2 %fusion.25 = bf16[256,2048]{1,0:T(8,128)(2,1)S(1)} fusion(bf16[2048,2048]{1,0:T(8,128)(2,1)} %param.17, bf16[40,2048]{1,0:T(8,128)(2,1)} %param.15, f32[2048]{0:T(1024)} %param.18, f32[2048]{0:T(1024)} %param.16, bf16[2048,40]{0,1:T(8,128)(2,1)} %param.14, s32[]{:T(128)S(6)} %select_n.12), kind=kOutput, calls=%fused_computation.33 | convolution fusion | flops 2192572416 | bytes 9637892 | tf_op jit(solution)/shard_map/dot_general | solution.py:20
  22.0 11.2 %all-to-all-start.1 = ((s32[128,4,1]{1,2,0:T(1,128)}), s32[128,4,1]{1,2,0:T(1,128)S(1)}, u32[]{:S(2)}, u32[]{:S(2)}) async-start(s32[128,4,1]{1,2,0:T(1,128)} %bitcast.3), calls=%async_computation.1 | async-start | bytes 131072 | tf_op jit(solution)/shard_map/all_to_all | solution.py:55
  33.2 9.0 %maximum_convert_fusion = bf16[512,2048]{1,0:T(8,128)(2,1)} fusion(bf16[2048,2048]{1,0:T(8,128)(2,1)} %param.17, f32[2048]{0:T(1024)S(1)} %copy-done.7, bf16[512,40]{0,1:T(8,128)(2,1)S(1)} %copy-done.6, bf16[40,2048]{1,0:T(8,128)(2,1)S(1)} %copy-done.5, f32[2048]{0:T(1024)S(1)} %copy-done.8), kind=kOutput, calls=%fused_computation.26 | convolution fusion | flops 4385144832 | bytes 10706944 | tf_op jit(solution)/shard_map/dot_general | solution.py:20
  47.3 9.8 %all-to-all-start = ((bf16[128,4,256]{2,1,0:T(4,128)(2,1)}), bf16[128,4,256]{2,1,0:T(4,128)(2,1)S(1)}, u32[]{:S(2)}, u32[]{:S(2)}) async-start(bf16[128,4,256]{2,1,0:T(4,128)(2,1)} %all_to_all.16), calls=%async_computation | async-start | bytes 524288 | tf_op jit(solution)/shard_map/all_to_all | solution.py:54
  62.3 5.4 %all-to-all-done = bf16[128,4,256]{2,1,0:T(4,128)(2,1)S(1)} async-done(((bf16[128,4,256]{2,1,0:T(4,128)(2,1)}), bf16[128,4,256]{2,1,0:T(4,128)(2,1)S(1)}, u32[]{:S(2)}, u32[]{:S(2)}) %all-to-all-start) | async-done | bytes 262176 | tf_op jit(solution)/shard_map/all_to_all | solution.py:54
  72.3 31.6 %all-gather.6.cloned.1.call-done = bf16[8192,256]{1,0:T(8,128)(2,1)} async-done(((bf16[512,256]{1,0:T(8,128)(2,1)}), bf16[8192,256]{1,0:T(8,128)(2,1)}) %all-gather.6.cloned.1.call-update) | async-done | bytes 4194320 | tf_op jit(solution)/shard_map/all_gather | solution.py:58
  103.8 5.6 %fusion.21 = (bf16[8192,256]{1,0:T(8,128)(2,1)}, f32[8192]{0:T(1024)S(1)}) fusion(bf16[8192,256]{1,0:T(8,128)(2,1)} %all-gather.6.cloned.1.call-done, f32[256]{0:T(256)S(1)} %copy-done.3), kind=kLoop, calls=%fused_computation.25 | loop fusion | flops 12574720 | bytes 8422400 | tf_op jit(solution)/shard_map/convert_element_type | solution.py:65
  109.5 170.4 %while.10 = (s32[]{:T(128)}, f32[16,512,64]{1,0,2:T(8,128)}, f32[16,512]{1,0:T(8,128)S(1)}, f32[2048]{0:T(1024)S(1)}, bf16[16,512,256]{2,1,0:T(8,128)(2,1)}, /*i...) while((s32[]{:T(128)}, f32[16,512,64]{1,0,2:T(8,128)}, ...), condition=%wide.region_5.6_spmd, body=%wide.region_4.5_spmd.sunk | while | flops 1346371584 | bytes 10893925 | solution.py:90
  121.9 5.0 %fusion.56 = f32[1,512,64]{1,2,0:T(8,128)S(1)} fusion(f32[2048,64]{0,1:T(8,128)S(1)} %get-tuple-element.130, f32[512,2048]{1,0:T(8,128)S(1)} %fusion.55, f32[2048]{0:T(1024)S(1)} %get-tuple-element.127, f32[512]{0:T(512)S(1)} %bitcast.37), kind=kOutput, calls=%fused_computation.13.clone.1 | convolution fusion | flops 809500672 | bytes 4859904 | tf_op jit(solution)/shard_map/while/body/eval_jaxpr/dot_general | solution.py:86
  132.5 5.0 %fusion.56 = f32[1,512,64]{1,2,0:T(8,128)S(1)} fusion(f32[2048,64]{0,1:T(8,128)S(1)} %get-tuple-element.130, f32[512,2048]{1,0:T(8,128)S(1)} %fusion.55, f32[2048]{0:T(1024)S(1)} %get-tuple-element.127, f32[512]{0:T(512)S(1)} %bitcast.37), kind=kOutput, calls=%fused_computation.13.clone.1 | convolution fusion | flops 809500672 | bytes 4859904 | tf_op jit(solution)/shard_map/while/body/eval_jaxpr/dot_general | solution.py:86
  143.1 5.0 %fusion.56 = f32[1,512,64]{1,2,0:T(8,128)S(1)} fusion(f32[2048,64]{0,1:T(8,128)S(1)} %get-tuple-element.130, f32[512,2048]{1,0:T(8,128)S(1)} %fusion.55, f32[2048]{0:T(1024)S(1)} %get-tuple-element.127, f32[512]{0:T(512)S(1)} %bitcast.37), kind=kOutput, calls=%fused_computation.13.clone.1 | convolution fusion | flops 809500672 | bytes 4859904 | tf_op jit(solution)/shard_map/while/body/eval_jaxpr/dot_general | solution.py:86
  153.8 5.0 %fusion.56 = f32[1,512,64]{1,2,0:T(8,128)S(1)} fusion(f32[2048,64]{0,1:T(8,128)S(1)} %get-tuple-element.130, f32[512,2048]{1,0:T(8,128)S(1)} %fusion.55, f32[2048]{0:T(1024)S(1)} %get-tuple-element.127, f32[512]{0:T(512)S(1)} %bitcast.37), kind=kOutput, calls=%fused_computation.13.clone.1 | convolution fusion | flops 809500672 | bytes 4859904 | tf_op jit(solution)/shard_map/while/body/eval_jaxpr/dot_general | solution.py:86
  164.4 5.0 %fusion.56 = f32[1,512,64]{1,2,0:T(8,128)S(1)} fusion(f32[2048,64]{0,1:T(8,128)S(1)} %get-tuple-element.130, f32[512,2048]{1,0:T(8,128)S(1)} %fusion.55, f32[2048]{0:T(1024)S(1)} %get-tuple-element.127, f32[512]{0:T(512)S(1)} %bitcast.37), kind=kOutput, calls=%fused_computation.13.clone.1 | convolution fusion | flops 809500672 | bytes 4859904 | tf_op jit(solution)/shard_map/while/body/eval_jaxpr/dot_general | solution.py:86
  175.1 5.0 %fusion.56 = f32[1,512,64]{1,2,0:T(8,128)S(1)} fusion(f32[2048,64]{0,1:T(8,128)S(1)} %get-tuple-element.130, f32[512,2048]{1,0:T(8,128)S(1)} %fusion.55, f32[2048]{0:T(1024)S(1)} %get-tuple-element.127, f32[512]{0:T(512)S(1)} %bitcast.37), kind=kOutput, calls=%fused_computation.13.clone.1 | convolution fusion | flops 809500672 | bytes 4859904 | tf_op jit(solution)/shard_map/while/body/eval_jaxpr/dot_general | solution.py:86
  185.7 5.0 %fusion.56 = f32[1,512,64]{1,2,0:T(8,128)S(1)} fusion(f32[2048,64]{0,1:T(8,128)S(1)} %get-tuple-element.130, f32[512,2048]{1,0:T(8,128)S(1)} %fusion.55, f32[2048]{0:T(1024)S(1)} %get-tuple-element.127, f32[512]{0:T(512)S(1)} %bitcast.37), kind=kOutput, calls=%fused_computation.13.clone.1 | convolution fusion | flops 809500672 | bytes 4859904 | tf_op jit(solution)/shard_map/while/body/eval_jaxpr/dot_general | solution.py:86
  196.4 5.0 %fusion.56 = f32[1,512,64]{1,2,0:T(8,128)S(1)} fusion(f32[2048,64]{0,1:T(8,128)S(1)} %get-tuple-element.130, f32[512,2048]{1,0:T(8,128)S(1)} %fusion.55, f32[2048]{0:T(1024)S(1)} %get-tuple-element.127, f32[512]{0:T(512)S(1)} %bitcast.37), kind=kOutput, calls=%fused_computation.13.clone.1 | convolution fusion | flops 809500672 | bytes 4859904 | tf_op jit(solution)/shard_map/while/body/eval_jaxpr/dot_general | solution.py:86
  207.0 5.0 %fusion.56 = f32[1,512,64]{1,2,0:T(8,128)S(1)} fusion(f32[2048,64]{0,1:T(8,128)S(1)} %get-tuple-element.130, f32[512,2048]{1,0:T(8,128)S(1)} %fusion.55, f32[2048]{0:T(1024)S(1)} %get-tuple-element.127, f32[512]{0:T(512)S(1)} %bitcast.37), kind=kOutput, calls=%fused_computation.13.clone.1 | convolution fusion | flops 809500672 | bytes 4859904 | tf_op jit(solution)/shard_map/while/body/eval_jaxpr/dot_general | solution.py:86
  217.7 5.0 %fusion.56 = f32[1,512,64]{1,2,0:T(8,128)S(1)} fusion(f32[2048,64]{0,1:T(8,128)S(1)} %get-tuple-element.130, f32[512,2048]{1,0:T(8,128)S(1)} %fusion.55, f32[2048]{0:T(1024)S(1)} %get-tuple-element.127, f32[512]{0:T(512)S(1)} %bitcast.37), kind=kOutput, calls=%fused_computation.13.clone.1 | convolution fusion | flops 809500672 | bytes 4859904 | tf_op jit(solution)/shard_map/while/body/eval_jaxpr/dot_general | solution.py:86
  228.3 5.0 %fusion.56 = f32[1,512,64]{1,2,0:T(8,128)S(1)} fusion(f32[2048,64]{0,1:T(8,128)S(1)} %get-tuple-element.130, f32[512,2048]{1,0:T(8,128)S(1)} %fusion.55, f32[2048]{0:T(1024)S(1)} %get-tuple-element.127, f32[512]{0:T(512)S(1)} %bitcast.37), kind=kOutput, calls=%fused_computation.13.clone.1 | convolution fusion | flops 809500672 | bytes 4859904 | tf_op jit(solution)/shard_map/while/body/eval_jaxpr/dot_general | solution.py:86
  239.0 5.0 %fusion.56 = f32[1,512,64]{1,2,0:T(8,128)S(1)} fusion(f32[2048,64]{0,1:T(8,128)S(1)} %get-tuple-element.130, f32[512,2048]{1,0:T(8,128)S(1)} %fusion.55, f32[2048]{0:T(1024)S(1)} %get-tuple-element.127, f32[512]{0:T(512)S(1)} %bitcast.37), kind=kOutput, calls=%fused_computation.13.clone.1 | convolution fusion | flops 809500672 | bytes 4859904 | tf_op jit(solution)/shard_map/while/body/eval_jaxpr/dot_general | solution.py:86
  249.6 5.0 %fusion.56 = f32[1,512,64]{1,2,0:T(8,128)S(1)} fusion(f32[2048,64]{0,1:T(8,128)S(1)} %get-tuple-element.130, f32[512,2048]{1,0:T(8,128)S(1)} %fusion.55, f32[2048]{0:T(1024)S(1)} %get-tuple-element.127, f32[512]{0:T(512)S(1)} %bitcast.37), kind=kOutput, calls=%fused_computation.13.clone.1 | convolution fusion | flops 809500672 | bytes 4859904 | tf_op jit(solution)/shard_map/while/body/eval_jaxpr/dot_general | solution.py:86
  260.3 5.0 %fusion.56 = f32[1,512,64]{1,2,0:T(8,128)S(1)} fusion(f32[2048,64]{0,1:T(8,128)S(1)} %get-tuple-element.130, f32[512,2048]{1,0:T(8,128)S(1)} %fusion.55, f32[2048]{0:T(1024)S(1)} %get-tuple-element.127, f32[512]{0:T(512)S(1)} %bitcast.37), kind=kOutput, calls=%fused_computation.13.clone.1 | convolution fusion | flops 809500672 | bytes 4859904 | tf_op jit(solution)/shard_map/while/body/eval_jaxpr/dot_general | solution.py:86
  270.9 5.0 %fusion.56 = f32[1,512,64]{1,2,0:T(8,128)S(1)} fusion(f32[2048,64]{0,1:T(8,128)S(1)} %get-tuple-element.130, f32[512,2048]{1,0:T(8,128)S(1)} %fusion.55, f32[2048]{0:T(1024)S(1)} %get-tuple-element.127, f32[512]{0:T(512)S(1)} %bitcast.37), kind=kOutput, calls=%fused_computation.13.clone.1 | convolution fusion | flops 809500672 | bytes 4859904 | tf_op jit(solution)/shard_map/while/body/eval_jaxpr/dot_general | solution.py:86
  284.1 64.3 %reduce-scatter.2.cloned.1.call-done = f32[512,64]{0,1:T(8,128)} async-done(((f32[8192,64]{0,1:T(8,128)}), f32[512,64]{0,1:T(8,128)}) %reduce-scatter.2.cloned.1.call-update) | async-done | bytes 131088 | tf_op jit(solution)/shard_map/reduce_scatter | solution.py:92
  (114 shorter events, 123.2 us)
Async XLA Ops:
  6.5 6.2 %copy-start = (bf16[2048,256]{1,0:T(8,128)(2,1)S(1)}, bf16[2048,256]{1,0:T(8,128)(2,1)}, u32[]{:S(2)}) copy-start(bf16[2048,256]{1,0:T(8,128)(2,1)} %param.19) | copy-start | bytes 3145732
  6.5 64.1 %all-gather.4.cloned.1.call-start = ((), (), s32[]{:S(2)}) async-start(), calls=%async_computation.3 | async-start | bytes 1179648 | tf_op jit(solution)/shard_map/all_gather | solution.py:77
  6.5 7.4 %copy-start.1 = (s32[512]{0:T(512)S(1)}, s32[512]{0:T(512)}, u32[]{:S(2)}) copy-start(s32[512]{0:T(512)} %param.13) | copy-start | bytes 6148
  12.8 20.4 %copy-start.5 = (bf16[40,2048]{1,0:T(8,128)(2,1)S(1)}, bf16[40,2048]{1,0:T(8,128)(2,1)}, u32[]{:S(2)}) copy-start(bf16[40,2048]{1,0:T(8,128)(2,1)} %param.15) | copy-start | bytes 491524
  12.8 20.4 %copy-start.6 = (bf16[512,40]{0,1:T(8,128)(2,1)S(1)}, bf16[512,40]{0,1:T(8,128)(2,1)}, u32[]{:S(2)}) copy-start(bf16[512,40]{0,1:T(8,128)(2,1)} %param.12) | copy-start | bytes 122884
  12.8 20.4 %copy-start.7 = (f32[2048]{0:T(1024)S(1)}, f32[2048]{0:T(1024)}, u32[]{:S(2)}) copy-start(f32[2048]{0:T(1024)} %param.18) | copy-start | bytes 24580
  12.8 20.4 %copy-start.8 = (f32[2048]{0:T(1024)S(1)}, f32[2048]{0:T(1024)}, u32[]{:S(2)}) copy-start(f32[2048]{0:T(1024)} %param.16) | copy-start | bytes 24580
  22.0 25.3 %all-to-all-start.1 = ((s32[128,4,1]{1,2,0:T(1,128)}), s32[128,4,1]{1,2,0:T(1,128)S(1)}, u32[]{:S(2)}, u32[]{:S(2)}) async-start(s32[128,4,1]{1,2,0:T(1,128)} %bitcast.3), calls=%async_computation.1 | async-start | bytes 131072 | tf_op jit(solution)/shard_map/all_to_all | solution.py:55
  44.5 26.1 %copy-start.3 = (f32[256]{0:T(256)S(1)}, f32[256]{0:T(256)}, u32[]{:S(2)}) copy-start(f32[256]{0:T(256)} %param.20) | copy-start | bytes 3076
  47.3 20.5 %all-to-all-start = ((bf16[128,4,256]{2,1,0:T(4,128)(2,1)}), bf16[128,4,256]{2,1,0:T(4,128)(2,1)S(1)}, u32[]{:S(2)}, u32[]{:S(2)}) async-start(bf16[128,4,256]{2,1,0:T(4,128)(2,1)} %all_to_all.16), calls=%async_computation | async-start | bytes 524288 | tf_op jit(solution)/shard_map/all_to_all | solution.py:54
  57.0 46.8 %all-gather.6.cloned.1.call-start = ((), (), s32[]{:S(2)}) async-start(), calls=%async_computation.5 | async-start | bytes 4456448 | tf_op jit(solution)/shard_map/all_gather | solution.py:58
  70.4 278.0 %reduce-scatter.2.cloned.1.call-start = ((), (), s32[]{:S(2)}) async-start(), calls=%async_computation.4 | async-start | bytes 2228224 | tf_op jit(solution)/shard_map/reduce_scatter | solution.py:92
  72.3 37.2 %copy-start.2 = (bf16[2048,256]{1,0:T(8,128)(2,1)S(1)}, bf16[2048,256]{1,0:T(8,128)(2,1)}, u32[]{:S(2)}) copy-start(bf16[2048,256]{1,0:T(8,128)(2,1)} %all-gather.4.cloned.1.call-done) | copy-start | bytes 3145732
  72.3 37.2 %copy-start.4 = (f32[2048,64]{0,1:T(8,128)S(1)}, f32[2048,64]{0,1:T(8,128)}, u32[]{:S(2)}) copy-start(f32[2048,64]{0,1:T(8,128)} %param.21) | copy-start | bytes 1572868
Sparse Core Ops, SparseCore 0:
  14.1 50.4 all-gather.3
  70.5 33.2 all-gather.5
  284.2 64.1 reduce-scatter.1
where the time goes:
time: 357 us; the launch traced here: 355 us
  matrix products  126 us (35%)
  waiting for transfers between devices  101 us (28%)
  local copies, waits for them, and re-layouts  77.6 us (22%)
  starting transfers between devices  21.2 us (6%)
  other arithmetic  15.6 us (4%)
  between operations  13.3 us (4%)
    dot_general x16, matrix products, one_block(): jnp.dot(kern, probes, precision=lax.Precision.HIGHEST, preferred_element_...  79.9 us
    reduce_scatter x1, waiting for transfers between devices, per_device(): lax.psum_scatter(partial_sums, 'col', scatter_dimension=0, tiled=True)  64.3 us
    dynamic_update_slice x32, local copies, waits for them, and re-layouts, per_device(): added = lax.map(one_block, (scaled, sq_row))  62.9 us
    all_gather x1, waiting for transfers between devices, per_device(): row_feature_matrix = lax.all_gather(placed, 'col', axis=0, tiled=True)  31.6 us
    dot_general x16, matrix products, one_block(): lax.dot_general(scaled_rows, piece, (((1,), (1,)), ((), ())), preferred_e...  27 us
    dot_general x2, matrix products, feature_extractor(): jnp.dot(hidden, middle_layer_weight, preferred_element_type=jnp.float32)  15.2 us
    all_to_all x1, starting transfers between devices, per_device(): lax.all_to_all(sent_ids, ('row', 'col'), split_axis=0, concat_axis=0, til...  11.2 us
    all_to_all x1, starting transfers between devices, per_device(): lax.all_to_all(feature_matrix, ('row', 'col'), split_axis=0, concat_axis=...  9.75 us
  transfers between devices with their start and end apart: 5, of which 3 were waited for; matrix products, arithmetic and copies ran while one was open for 8% of the time, Pallas kernels for 0%

commit v1 on v0

--- a/solution.py
+++ b/solution.py
@@ -55,7 +55,9 @@
         lax.all_to_all(sent_ids, ("row", "col"), split_axis=0, concat_axis=0, tiled=True),
     )
     placed = got_feats[jnp.argsort(got_ids)]
-    row_feature_matrix = lax.all_gather(placed, "col", axis=0, tiled=True)
+    row_feature_matrix = jnp.concatenate(
+        lax.all_to_all(jnp.stack([placed] * lax.axis_size("col")), "col", 0, 0), axis=0
+    )
     row_total = row_feature_matrix.shape[0]
     block_rows = min(512, row_total)
     blocks = row_total // block_rows

time: 357 us -> 392 us (1.098)
  waiting for transfers between devices: 101 us -> 129 us
  starting transfers between devices: 21.2 us -> 25.9 us
    all_gather x1, waiting for transfers between devices: 0.02 us -> 60.2 us  [per_device(): piece = lax.all_gather(col_feats, 'row', axis=0, tiled=True)]
    all_gather x1 -> x0, waiting for transfers between devices: 31.6 us -> none  [per_device(): row_feature_matrix = lax.all_gather(placed, 'col', axis=0, tiled=True)]
    all_to_all x0 -> x1, starting transfers between devices: none -> 4.66 us  [per_device(): lax.all_to_all(jnp.stack([placed] * lax.axis_size('col')), 'col', 0, 0)]
  transfers between devices with their start and end apart: 5 -> 5, of which waited for: 3 -> 3; matrix products, arithmetic and copies ran while one was open for 8% -> 7% of each run, Pallas kernels for 0% -> 0%
where the time goes in v1:
time: 392 us; the launch traced here: 390 us
  waiting for transfers between devices  129 us (33%)
  matrix products  125 us (32%)
  local copies, waits for them, and re-layouts  79.3 us (20%)
  starting transfers between devices  25.9 us (7%)
  other arithmetic  16.4 us (4%)
  between operations  13.6 us (3%)
    dot_general x16, matrix products, one_block(): jnp.dot(kern, probes, precision=lax.Precision.HIGHEST, preferred_element_...  79.9 us
    reduce_scatter x1, waiting for transfers between devices, per_device(): lax.psum_scatter(partial_sums, 'col', scatter_dimension=0, tiled=True)  63.1 us
    dynamic_update_slice x32, local copies, waits for them, and re-layouts, per_device(): added = lax.map(one_block, (scaled, sq_row))  62.9 us
    all_gather x1, waiting for transfers between devices, per_device(): piece = lax.all_gather(col_feats, 'row', axis=0, tiled=True)  60.2 us
    dot_general x16, matrix products, one_block(): lax.dot_general(scaled_rows, piece, (((1,), (1,)), ((), ())), preferred_e...  27 us
    dot_general x2, matrix products, feature_extractor(): jnp.dot(hidden, middle_layer_weight, preferred_element_type=jnp.float32)  15.1 us
    all_to_all x1, starting transfers between devices, per_device(): lax.all_to_all(sent_ids, ('row', 'col'), split_axis=0, concat_axis=0, til...  11.2 us
    all_to_all x1, starting transfers between devices, per_device(): lax.all_to_all(feature_matrix, ('row', 'col'), split_axis=0, concat_axis=...  9.76 us
  transfers between devices with their start and end apart: 5, of which 3 were waited for; matrix products, arithmetic and copies ran while one was open for 7% of the time, Pallas kernels for 0%

profile of v1, /device:TPU:0, one launch (start us, length us, event | category | flops | bytes accessed | tf_op | source)
XLA Modules:
  0.0 389.8 jit_solution(10322667532879915275)
XLA Ops:
  15.4 11.2 %all-to-all-start.1 = ((s32[128,4,1]{1,2,0:T(1,128)}), s32[128,4,1]{1,2,0:T(1,128)S(1)}, u32[]{:S(2)}, u32[]{:S(2)}) async-start(s32[128,4,1]{1,2,0:T(1,128)} %bitcast.3), calls=%async_computation.1 | async-start | bytes 131072 | tf_op jit(solution)/shard_map/all_to_all | solution.py:55
  26.6 9.1 %maximum_convert_fusion = bf16[512,2048]{1,0:T(8,128)(2,1)} fusion(bf16[2048,2048]{1,0:T(8,128)(2,1)} %param.17, f32[2048]{0:T(1024)} %param.18, bf16[512,40]{0,1:T(8,128)(2,1)} %param.12, bf16[40,2048]{1,0:T(8,128)(2,1)} %param.15, f32[2048]{0:T(1024)} %param.16), kind=kOutput, calls=%fused_computation.26 | convolution fusion | flops 4385144832 | bytes 10706944 | tf_op jit(solution)/shard_map/dot_general | solution.py:20
  40.7 9.8 %all-to-all-start = ((bf16[128,4,256]{2,1,0:T(4,128)(2,1)}), bf16[128,4,256]{2,1,0:T(4,128)(2,1)S(1)}, u32[]{:S(2)}, u32[]{:S(2)}) async-start(bf16[128,4,256]{2,1,0:T(4,128)(2,1)} %all_to_all.19), calls=%async_computation | async-start | bytes 524288 | tf_op jit(solution)/shard_map/all_to_all | solution.py:54
  55.7 5.5 %all-to-all-done = bf16[128,4,256]{2,1,0:T(4,128)(2,1)S(1)} async-done(((bf16[128,4,256]{2,1,0:T(4,128)(2,1)}), bf16[128,4,256]{2,1,0:T(4,128)(2,1)S(1)}, u32[]{:S(2)}, u32[]{:S(2)}) %all-to-all-start) | async-done | bytes 262176 | tf_op jit(solution)/shard_map/all_to_all | solution.py:54
  70.3 6.0 %fusion.25 = bf16[256,2048]{1,0:T(8,128)(2,1)S(1)} fusion(bf16[2048,2048]{1,0:T(8,128)(2,1)} %param.17, bf16[40,2048]{1,0:T(8,128)(2,1)S(1)} %copy-done.4, f32[2048]{0:T(1024)S(1)} %copy-done.5, f32[2048]{0:T(1024)S(1)} %copy-done.6, bf16[2048,40]{0,1:T(8,128)(2,1)} %param.14, s32[]{:T(128)S(6)} %select_n.12), kind=kOutput, calls=%fused_computation.33 | convolution fusion | flops 2192572416 | bytes 9637892 | tf_op jit(solution)/shard_map/dot_general | solution.py:20
  77.7 60.2 %all-gather.2.cloned.1.call-done = bf16[2048,256]{1,0:T(8,128)(2,1)} async-done(((bf16[256,256]{1,0:T(8,128)(2,1)}), bf16[2048,256]{1,0:T(8,128)(2,1)}) %all-gather.2.cloned.1.call-update) | async-done | bytes 1048592 | tf_op jit(solution)/shard_map/all_gather | solution.py:79
  139.5 5.7 %fusion.21 = (bf16[16,512,256]{2,1,0:T(8,128)(2,1)}, f32[16,512]{1,0:T(8,128)S(1)}) fusion(bf16[16,512,256]{2,1,0:T(8,128)(2,1)} %all-to-all-done.2, f32[256]{0:T(256)S(1)} %copy-done.2), kind=kLoop, calls=%fused_computation.25 | loop fusion | flops 12574720 | bytes 8422400 | tf_op jit(solution)/shard_map/convert_element_type | solution.py:67
  145.3 170.4 %while.10 = (s32[]{:T(128)}, f32[16,512,64]{1,0,2:T(8,128)}, f32[16,512]{1,0:T(8,128)S(1)}, f32[2048]{0:T(1024)S(1)}, bf16[16,512,256]{2,1,0:T(8,128)(2,1)}, /*i...) while((s32[]{:T(128)}, f32[16,512,64]{1,0,2:T(8,128)}, ...), condition=%wide.region_5.6_spmd, body=%wide.region_4.5_spmd.sunk | while | flops 1346371584 | bytes 10893925 | solution.py:92
  147.0 5.0 %fusion.56 = f32[1,512,64]{1,2,0:T(8,128)S(1)} fusion(f32[2048,64]{0,1:T(8,128)S(1)} %get-tuple-element.130, f32[512,2048]{1,0:T(8,128)S(1)} %fusion.55, f32[2048]{0:T(1024)S(1)} %get-tuple-element.127, f32[512]{0:T(512)S(1)} %bitcast.35), kind=kOutput, calls=%fused_computation.13.clone.1 | convolution fusion | flops 809500672 | bytes 4859904 | tf_op jit(solution)/shard_map/while/body/eval_jaxpr/dot_general | solution.py:88
  157.6 5.0 %fusion.56 = f32[1,512,64]{1,2,0:T(8,128)S(1)} fusion(f32[2048,64]{0,1:T(8,128)S(1)} %get-tuple-element.130, f32[512,2048]{1,0:T(8,128)S(1)} %fusion.55, f32[2048]{0:T(1024)S(1)} %get-tuple-element.127, f32[512]{0:T(512)S(1)} %bitcast.35), kind=kOutput, calls=%fused_computation.13.clone.1 | convolution fusion | flops 809500672 | bytes 4859904 | tf_op jit(solution)/shard_map/while/body/eval_jaxpr/dot_general | solution.py:88
  168.3 5.0 %fusion.56 = f32[1,512,64]{1,2,0:T(8,128)S(1)} fusion(f32[2048,64]{0,1:T(8,128)S(1)} %get-tuple-element.130, f32[512,2048]{1,0:T(8,128)S(1)} %fusion.55, f32[2048]{0:T(1024)S(1)} %get-tuple-element.127, f32[512]{0:T(512)S(1)} %bitcast.35), kind=kOutput, calls=%fused_computation.13.clone.1 | convolution fusion | flops 809500672 | bytes 4859904 | tf_op jit(solution)/shard_map/while/body/eval_jaxpr/dot_general | solution.py:88
  178.9 5.0 %fusion.56 = f32[1,512,64]{1,2,0:T(8,128)S(1)} fusion(f32[2048,64]{0,1:T(8,128)S(1)} %get-tuple-element.130, f32[512,2048]{1,0:T(8,128)S(1)} %fusion.55, f32[2048]{0:T(1024)S(1)} %get-tuple-element.127, f32[512]{0:T(512)S(1)} %bitcast.35), kind=kOutput, calls=%fused_computation.13.clone.1 | convolution fusion | flops 809500672 | bytes 4859904 | tf_op jit(solution)/shard_map/while/body/eval_jaxpr/dot_general | solution.py:88
  189.6 5.0 %fusion.56 = f32[1,512,64]{1,2,0:T(8,128)S(1)} fusion(f32[2048,64]{0,1:T(8,128)S(1)} %get-tuple-element.130, f32[512,2048]{1,0:T(8,128)S(1)} %fusion.55, f32[2048]{0:T(1024)S(1)} %get-tuple-element.127, f32[512]{0:T(512)S(1)} %bitcast.35), kind=kOutput, calls=%fused_computation.13.clone.1 | convolution fusion | flops 809500672 | bytes 4859904 | tf_op jit(solution)/shard_map/while/body/eval_jaxpr/dot_general | solution.py:88
  200.2 5.0 %fusion.56 = f32[1,512,64]{1,2,0:T(8,128)S(1)} fusion(f32[2048,64]{0,1:T(8,128)S(1)} %get-tuple-element.130, f32[512,2048]{1,0:T(8,128)S(1)} %fusion.55, f32[2048]{0:T(1024)S(1)} %get-tuple-element.127, f32[512]{0:T(512)S(1)} %bitcast.35), kind=kOutput, calls=%fused_computation.13.clone.1 | convolution fusion | flops 809500672 | bytes 4859904 | tf_op jit(solution)/shard_map/while/body/eval_jaxpr/dot_general | solution.py:88
  221.5 5.0 %fusion.56 = f32[1,512,64]{1,2,0:T(8,128)S(1)} fusion(f32[2048,64]{0,1:T(8,128)S(1)} %get-tuple-element.130, f32[512,2048]{1,0:T(8,128)S(1)} %fusion.55, f32[2048]{0:T(1024)S(1)} %get-tuple-element.127, f32[512]{0:T(512)S(1)} %bitcast.35), kind=kOutput, calls=%fused_computation.13.clone.1 | convolution fusion | flops 809500672 | bytes 4859904 | tf_op jit(solution)/shard_map/while/body/eval_jaxpr/dot_general | solution.py:88
  232.1 5.0 %fusion.56 = f32[1,512,64]{1,2,0:T(8,128)S(1)} fusion(f32[2048,64]{0,1:T(8,128)S(1)} %get-tuple-element.130, f32[512,2048]{1,0:T(8,128)S(1)} %fusion.55, f32[2048]{0:T(1024)S(1)} %get-tuple-element.127, f32[512]{0:T(512)S(1)} %bitcast.35), kind=kOutput, calls=%fused_computation.13.clone.1 | convolution fusion | flops 809500672 | bytes 4859904 | tf_op jit(solution)/shard_map/while/body/eval_jaxpr/dot_general | solution.py:88
  242.8 5.0 %fusion.56 = f32[1,512,64]{1,2,0:T(8,128)S(1)} fusion(f32[2048,64]{0,1:T(8,128)S(1)} %get-tuple-element.130, f32[512,2048]{1,0:T(8,128)S(1)} %fusion.55, f32[2048]{0:T(1024)S(1)} %get-tuple-element.127, f32[512]{0:T(512)S(1)} %bitcast.35), kind=kOutput, calls=%fused_computation.13.clone.1 | convolution fusion | flops 809500672 | bytes 4859904 | tf_op jit(solution)/shard_map/while/body/eval_jaxpr/dot_general | solution.py:88
  253.4 5.0 %fusion.56 = f32[1,512,64]{1,2,0:T(8,128)S(1)} fusion(f32[2048,64]{0,1:T(8,128)S(1)} %get-tuple-element.130, f32[512,2048]{1,0:T(8,128)S(1)} %fusion.55, f32[2048]{0:T(1024)S(1)} %get-tuple-element.127, f32[512]{0:T(512)S(1)} %bitcast.35), kind=kOutput, calls=%fused_computation.13.clone.1 | convolution fusion | flops 809500672 | bytes 4859904 | tf_op jit(solution)/shard_map/while/body/eval_jaxpr/dot_general | solution.py:88
  264.1 5.0 %fusion.56 = f32[1,512,64]{1,2,0:T(8,128)S(1)} fusion(f32[2048,64]{0,1:T(8,128)S(1)} %get-tuple-element.130, f32[512,2048]{1,0:T(8,128)S(1)} %fusion.55, f32[2048]{0:T(1024)S(1)} %get-tuple-element.127, f32[512]{0:T(512)S(1)} %bitcast.35), kind=kOutput, calls=%fused_computation.13.clone.1 | convolution fusion | flops 809500672 | bytes 4859904 | tf_op jit(solution)/shard_map/while/body/eval_jaxpr/dot_general | solution.py:88
  274.7 5.0 %fusion.56 = f32[1,512,64]{1,2,0:T(8,128)S(1)} fusion(f32[2048,64]{0,1:T(8,128)S(1)} %get-tuple-element.130, f32[512,2048]{1,0:T(8,128)S(1)} %fusion.55, f32[2048]{0:T(1024)S(1)} %get-tuple-element.127, f32[512]{0:T(512)S(1)} %bitcast.35), kind=kOutput, calls=%fused_computation.13.clone.1 | convolution fusion | flops 809500672 | bytes 4859904 | tf_op jit(solution)/shard_map/while/body/eval_jaxpr/dot_general | solution.py:88
  285.4 5.0 %fusion.56 = f32[1,512,64]{1,2,0:T(8,128)S(1)} fusion(f32[2048,64]{0,1:T(8,128)S(1)} %get-tuple-element.130, f32[512,2048]{1,0:T(8,128)S(1)} %fusion.55, f32[2048]{0:T(1024)S(1)} %get-tuple-element.127, f32[512]{0:T(512)S(1)} %bitcast.35), kind=kOutput, calls=%fused_computation.13.clone.1 | convolution fusion | flops 809500672 | bytes 4859904 | tf_op jit(solution)/shard_map/while/body/eval_jaxpr/dot_general | solution.py:88
  296.0 5.0 %fusion.56 = f32[1,512,64]{1,2,0:T(8,128)S(1)} fusion(f32[2048,64]{0,1:T(8,128)S(1)} %get-tuple-element.130, f32[512,2048]{1,0:T(8,128)S(1)} %fusion.55, f32[2048]{0:T(1024)S(1)} %get-tuple-element.127, f32[512]{0:T(512)S(1)} %bitcast.35), kind=kOutput, calls=%fused_computation.13.clone.1 | convolution fusion | flops 809500672 | bytes 4859904 | tf_op jit(solution)/shard_map/while/body/eval_jaxpr/dot_general | solution.py:88
  306.7 5.0 %fusion.56 = f32[1,512,64]{1,2,0:T(8,128)S(1)} fusion(f32[2048,64]{0,1:T(8,128)S(1)} %get-tuple-element.130, f32[512,2048]{1,0:T(8,128)S(1)} %fusion.55, f32[2048]{0:T(1024)S(1)} %get-tuple-element.127, f32[512]{0:T(512)S(1)} %bitcast.35), kind=kOutput, calls=%fused_computation.13.clone.1 | convolution fusion | flops 809500672 | bytes 4859904 | tf_op jit(solution)/shard_map/while/body/eval_jaxpr/dot_general | solution.py:88
  319.8 63.1 %reduce-scatter.2.cloned.1.call-done = f32[512,64]{0,1:T(8,128)} async-done(((f32[8192,64]{0,1:T(8,128)}), f32[512,64]{0,1:T(8,128)}) %reduce-scatter.2.cloned.1.call-update) | async-done | bytes 131088 | tf_op jit(solution)/shard_map/reduce_scatter | solution.py:94
  (109 shorter events, 130.4 us)
Async XLA Ops:
  6.5 29.2 %copy-start = (bf16[2048,256]{1,0:T(8,128)(2,1)S(1)}, bf16[2048,256]{1,0:T(8,128)(2,1)}, u32[]{:S(2)}) copy-start(bf16[2048,256]{1,0:T(8,128)(2,1)} %param.19) | copy-start | bytes 3145732
  15.4 25.3 %all-to-all-start.1 = ((s32[128,4,1]{1,2,0:T(1,128)}), s32[128,4,1]{1,2,0:T(1,128)S(1)}, u32[]{:S(2)}, u32[]{:S(2)}) async-start(s32[128,4,1]{1,2,0:T(1,128)} %bitcast.3), calls=%async_computation.1 | async-start | bytes 131072 | tf_op jit(solution)/shard_map/all_to_all | solution.py:55
  40.7 20.5 %all-to-all-start = ((bf16[128,4,256]{2,1,0:T(4,128)(2,1)}), bf16[128,4,256]{2,1,0:T(4,128)(2,1)S(1)}, u32[]{:S(2)}, u32[]{:S(2)}) async-start(bf16[128,4,256]{2,1,0:T(4,128)(2,1)} %all_to_all.19), calls=%async_computation | async-start | bytes 524288 | tf_op jit(solution)/shard_map/all_to_all | solution.py:54
  65.5 4.7 %copy-start.4 = (bf16[40,2048]{1,0:T(8,128)(2,1)S(1)}, bf16[40,2048]{1,0:T(8,128)(2,1)}, u32[]{:S(2)}) copy-start(bf16[40,2048]{1,0:T(8,128)(2,1)} %param.15) | copy-start | bytes 491524
  65.5 4.7 %copy-start.5 = (f32[2048]{0:T(1024)S(1)}, f32[2048]{0:T(1024)}, u32[]{:S(2)}) copy-start(f32[2048]{0:T(1024)} %param.18) | copy-start | bytes 24580
  65.5 4.7 %copy-start.6 = (f32[2048]{0:T(1024)S(1)}, f32[2048]{0:T(1024)}, u32[]{:S(2)}) copy-start(f32[2048]{0:T(1024)} %param.16) | copy-start | bytes 24580
  65.6 74.0 %all-to-all-start.2 = ((bf16[16,512,256]{2,1,0:T(8,128)(2,1)}), bf16[16,512,256]{2,1,0:T(8,128)(2,1)}, u32[]{:S(2)}, u32[]{:S(2)}) async-start(bf16[16,512,256]{2,1,0:T(8,128)(2,1)} %stack.2), calls=%async_computation.2 | async-start | bytes 8388608 | tf_op jit(solution)/shard_map/all_to_all | solution.py:59
  70.2 67.7 %all-gather.2.cloned.1.call-start = ((), (), s32[]{:S(2)}) async-start(), calls=%async_computation.4 | async-start | bytes 1179648 | tf_op jit(solution)/shard_map/all_gather | solution.py:79
  70.3 67.6 %copy-start.2 = (f32[256]{0:T(256)S(1)}, f32[256]{0:T(256)}, u32[]{:S(2)}) copy-start(f32[256]{0:T(256)} %param.20) | copy-start | bytes 3076
  77.5 305.5 %reduce-scatter.2.cloned.1.call-start = ((), (), s32[]{:S(2)}) async-start(), calls=%async_computation.5 | async-start | bytes 2228224 | tf_op jit(solution)/shard_map/reduce_scatter | solution.py:94
  139.5 5.8 %copy-start.1 = (bf16[2048,256]{1,0:T(8,128)(2,1)S(1)}, bf16[2048,256]{1,0:T(8,128)(2,1)}, u32[]{:S(2)}) copy-start(bf16[2048,256]{1,0:T(8,128)(2,1)} %all-gather.2.cloned.1.call-done) | copy-start | bytes 3145732
  139.5 5.8 %copy-start.3 = (f32[2048,64]{0,1:T(8,128)S(1)}, f32[2048,64]{0,1:T(8,128)}, u32[]{:S(2)}) copy-start(f32[2048,64]{0,1:T(8,128)} %param.21) | copy-start | bytes 1572868
Sparse Core Ops, SparseCore 0:
  77.6 60.2 all-gather.1
  320.0 62.9 reduce-scatter.1
